TPU v7x, 128 devices: a whole 4x4x4 slice. The times are simulated.
128 devices in a mesh: row: 8 (over x, core), mp: 16 (over y, z).
Axes of the slice: x: 4, y: 4, z: 4, core: 2. Of those that a mesh axis runs over, the one named last changes fastest.
Arguments:
- queries: bfloat16 [2560, 16384], P('row', 'mp'), may hold values from -16 to 16
- new_kv: bfloat16 [2560, 2048], P('row', 'mp'), may hold values from -9 to 9
- cache_keys: bfloat16 [512, 16, 512, 128], P('row', 'mp'), may hold values from -26 to 26
- cache_values: bfloat16 [512, 16, 512, 128], P('row', 'mp'), may hold values from -12 to 12
- cache_lens: int32 [512], P('row'), may hold values from 8 to 1019, as said below
- accepted: int32 [512], P('row'), may hold values from 0 to 5
- dest: int32 [512], P('row'), may hold values from 0 to 511, as said below
- out_weight: bfloat16 [16384, 16384], P('mp', 'row'), may hold values from -0.046875 to 0.046875
Outputs:
- mixed: bfloat16 [2560, 16384], P('mp', 'row')
- next_kv: bfloat16 [512, 5, 2048], P('row', None, 'mp')
Inputs may be any that keep to these rules, and one draw needn't show every extreme that they name: `cache_lens`: every beam's cache leaves room for its 5 new tokens. dest is a permutation of 0 to 511; of the beams in each aligned block of 64 beams, exactly 8 go to slots of each aligned block of 64 slots.
All inputs are finite; a program needn't handle non-finite values.
Results may differ from a plain program's by a relative error of at most 0.02.
Values may be sent and summed in bfloat16 or wider, within the bound.
A program may use at most 128 MiB of HBM per device.

v0:
```python
import jax
import jax.numpy as jnp
from jax import lax
from jax.sharding import PartitionSpec as P

masked_score = -1e30


def partner(block, axis, bit):
    count = lax.axis_size(axis)
    route = []
    for low in range(count):
        high = low | 1 << bit
        if high != low and high < count:
            route += [(low, high), (high, low)]
    return lax.ppermute(block, axis, route)


def head_slice(values, start, count):
    return lax.dynamic_slice_in_dim(values, start, count, 3)


def shards(queries, new_kv, cache_keys, cache_values, cache_lens, accepted, dest, out_weight):
    beams_here = cache_keys.shape[0]
    halves_held = cache_keys.shape[1]
    half_length = cache_keys.shape[2]
    head_size = cache_keys.shape[3]
    drafts = queries.shape[0] // beams_here
    heads_owned = queries.shape[1] // head_size
    kv_columns = new_kv.shape[1]
    mp_place = lax.axis_index("mp")
    lower_side = mp_place % 2 == 0
    partner_queries, partner_fresh = partner((queries, new_kv), "mp", 0)
    group_queries = jnp.where(
        lower_side,
        jnp.concatenate([queries, partner_queries], 1),
        jnp.concatenate([partner_queries, queries], 1),
    )
    fresh_pair = jnp.where(
        lower_side,
        jnp.concatenate([new_kv, partner_fresh], 1),
        jnp.concatenate([partner_fresh, new_kv], 1),
    )
    group_heads = group_queries.shape[1] // head_size
    sides = (mp_place * halves_held + jnp.arange(halves_held, dtype=jnp.int32)) % 2
    query_block = group_queries.reshape(beams_here, drafts, group_heads, head_size)
    fresh_block = fresh_pair.reshape(beams_here, drafts, 2, head_size)
    fresh_keys = fresh_block[:, :, 0]
    fresh_values = fresh_block[:, :, 1]
    scale = head_size ** (-0.5)
    cache_scores = (
        jnp.einsum("btjd,bsid->bstji", query_block, cache_keys, preferred_element_type=jnp.float32)
        * scale
    )
    fresh_scores = (
        jnp.einsum("btjd,bud->btju", query_block, fresh_keys, preferred_element_type=jnp.float32)
        * scale
    )
    spots = sides[:, None] * half_length + jnp.arange(half_length, dtype=jnp.int32)[None, :]
    cache_valid = (spots[None] < cache_lens[:, None, None])[:, :, None, None, :]
    order = jnp.arange(drafts, dtype=jnp.int32)
    fresh_side = (cache_lens[:, None] + order[None, :]) // half_length
    causal = order[:, None] >= order[None, :]
    fresh_valid = (
        causal[None, None] & (fresh_side[:, None, None, :] == sides[None, :, None, None])
    )[:, :, :, None, :]
    cache_masked = jnp.where(cache_valid, cache_scores, masked_score)
    fresh_masked = jnp.where(fresh_valid, fresh_scores[:, None], masked_score)
    highest = jnp.maximum(jnp.max(cache_masked, -1), jnp.max(fresh_masked, -1))
    cache_weights = jnp.where(cache_valid, jnp.exp(cache_masked - highest[..., None]), 0.0).astype(
        jnp.bfloat16
    )
    fresh_weights = jnp.where(fresh_valid, jnp.exp(fresh_masked - highest[..., None]), 0.0).astype(
        jnp.bfloat16
    )
    partial_value = jnp.einsum(
        "bstji,bsid->bstjd", cache_weights, cache_values, preferred_element_type=jnp.float32
    )
    partial_value = partial_value + jnp.einsum(
        "bstju,bud->bstjd", fresh_weights, fresh_values, preferred_element_type=jnp.float32
    )
    weight_mass = jnp.sum(cache_weights.astype(jnp.float32), -1) + jnp.sum(
        fresh_weights.astype(jnp.float32), -1
    )
    own_start = jnp.where(lower_side, 0, heads_owned).astype(jnp.int32)
    other_start = heads_owned - own_start
    got_partial, got_highest, got_mass = partner(
        (
            head_slice(partial_value, other_start, heads_owned),
            head_slice(highest, other_start, heads_owned),
            head_slice(weight_mass, other_start, heads_owned),
        ),
        "mp",
        0,
    )
    own_partial = head_slice(partial_value, own_start, heads_owned)
    own_highest = head_slice(highest, own_start, heads_owned)
    own_mass = head_slice(weight_mass, own_start, heads_owned)
    partial_value = jnp.where(
        lower_side,
        jnp.concatenate([own_partial, got_partial], 1),
        jnp.concatenate([got_partial, own_partial], 1),
    )
    highest = jnp.where(
        lower_side,
        jnp.concatenate([own_highest, got_highest], 1),
        jnp.concatenate([got_highest, own_highest], 1),
    )
    weight_mass = jnp.where(
        lower_side,
        jnp.concatenate([own_mass, got_mass], 1),
        jnp.concatenate([got_mass, own_mass], 1),
    )
    summit = jnp.max(highest, 1)
    factor = jnp.exp(highest - summit[:, None])
    numer = jnp.sum(factor[..., None] * partial_value, 1)
    denom = jnp.sum(factor * weight_mass, 1)
    attention = (
        (numer / denom[..., None])
        .astype(jnp.bfloat16)
        .reshape(beams_here * drafts, heads_owned * head_size)
    )
    projected = jnp.dot(
        lax.all_gather(attention, "row", axis=0, tiled=True),
        out_weight,
        preferred_element_type=jnp.float32,
    )
    rows_owned = projected.shape[0] // lax.axis_size("mp")
    totals = lax.psum(projected.astype(jnp.bfloat16), "mp").astype(jnp.float32)
    owned_rows = lax.dynamic_slice_in_dim(totals, mp_place * rows_owned, rows_owned, 0)
    mixed = owned_rows.astype(jnp.bfloat16)
    fresh_rows = new_kv.reshape(beams_here, drafts, kv_columns)
    kept_mask = order[None, :] < accepted[:, None]
    kept_rows = jnp.where(kept_mask[..., None], fresh_rows, jnp.zeros_like(fresh_rows)).reshape(
        beams_here, drafts * kv_columns
    )
    blocks = lax.axis_size("row")
    share_count = beams_here // blocks
    target = dest // beams_here
    landing = dest % beams_here
    beam_index = jnp.arange(beams_here, dtype=jnp.int32)
    earlier = (target[None, :] == target[:, None]) & (beam_index[None, :] < beam_index[:, None])
    position = jnp.sum(earlier.astype(jnp.int32), 1)
    send_slot = target * share_count + position
    picker = send_slot[None, :] == beam_index[:, None]
    outgoing = jnp.dot(
        picker.astype(jnp.bfloat16), kept_rows, preferred_element_type=jnp.float32
    ).astype(jnp.bfloat16)
    outgoing = outgoing.reshape(blocks, share_count, drafts * kv_columns)
    labels = jnp.sum(jnp.where(picker, landing[None, :], 0), 1).reshape(blocks, share_count)
    arrived, arrived_labels = (
        lax.all_to_all(outgoing, "row", split_axis=0, concat_axis=0, tiled=True),
        lax.all_to_all(labels, "row", split_axis=0, concat_axis=0, tiled=True),
    )
    arrived = arrived.reshape(beams_here, drafts * kv_columns)
    arrived_labels = arrived_labels.reshape(beams_here)
    placer = (arrived_labels[None, :] == beam_index[:, None]).astype(jnp.bfloat16)
    next_kv = jnp.dot(placer, arrived, preferred_element_type=jnp.float32).astype(jnp.bfloat16)
    next_kv = next_kv.reshape(beams_here, drafts, kv_columns)
    return (mixed, next_kv)


def solution(mesh):
    placed = (
        P("row", "mp"),
        P("row", "mp"),
        P("row", "mp", None, None),
        P("row", "mp", None, None),
        P("row"),
        P("row"),
        P("row"),
        P("mp", "row"),
    )
    return jax.shard_map(
        shards,
        mesh=mesh,
        in_specs=placed,
        out_specs=(P("mp", "row"), P("row", None, "mp")),
        check_vma=False,
    )
```

profile of v0, /device:TPU:1, one launch (start us, length us, event | category | flops | bytes accessed | tf_op | source)
XLA Modules:
  0.0 307.1 jit_solution(3005448129393214941)
XLA Ops:
  7.2 2.5 collective-permute-start
  9.9 0.7 fusion.18
  10.7 0.7 broadcast_compare_fusion
  11.4 14.7 %collective-permute-done.1 = bf16[320,128]{1,0:T(8,128)(2,1)S(1)} collective-permute-done((bf16[320,128]{1,0:T(8,128)(2,1)}, bf16[320,128]{1,0:T(8,128)(2,1)S(1)}, u32[]{:S(2)}, u32[]{:S(2)}) %collective-permute-start.1) | collective-permute-done | bytes 81952 | tf_op jit(solution)/shard_map/ppermute | solution.py:16
  26.2 1.0 maximum_select_fusion.2
  27.2 0.2 fusion.26
  27.5 1.8 fusion.10
  29.3 0.3 copy.56
  29.6 6.5 %fusion.1 = (f32[64,5,16]{2,1,0:T(8,128)S(1)}, f32[64,5,16,512]{3,2,1,0:T(8,128)S(1)}) fusion(pred[64,512]{1,0:T(8,128)(4,1)S(1)} %broadcast_compare_fusion, bf16[64,5,16,128]{3,2,1,0:T(8,128)(2,1)S(1)} %bitcast.96, bf16[64,1,512,128]{3,2,1,0:T(8,128)(2,1)} %param.10), kind=kOutput, calls=%fused_computation.5 | convolution fusion | flops 678947840 | bytes 20238336 | tf_op jit(solution)/shard_map/btjd,bsid->bstji/dot_general | solution.py:52
  36.1 3.2 %fusion.27 = (f32[64,5,16]{2,1,0:T(8,128)S(1)}, f32[64,5,16,5]{2,3,1,0:T(8,128)S(1)}) fusion(bf16[64,5,16,128]{3,2,1,0:T(8,128)(2,1)S(1)} %bitcast.97, bf16[64,5,1,128]{3,2,1,0:T(2,128)(2,1)S(1)} %get-tuple-element.23, pred[64,5,5]{2,1,0:T(8,128)(4,1)S(1)} %broadcast_and_fusion), kind=kOutput, calls=%fused_computation.78 | convolution fusion | flops 6625280 | bytes 1517120 | tf_op jit(solution)/shard_map/btjd,bud->btju/dot_general | solution.py:56
  39.3 1.5 convert_reduce_fusion.1
  40.8 5.6 %fusion.2 = f32[64,5,16,128]{3,2,1,0:T(8,128)S(1)} fusion(bf16[64,1,512,128]{3,2,1,0:T(8,128)(2,1)} %param.11, f32[64,5,16,512]{3,2,1,0:T(8,128)S(1)} %get-tuple-element.27, f32[64,5,16]{2,1,0:T(8,128)S(1)} %max.16, pred[64,512]{1,0:T(8,128)(4,1)S(1)} %broadcast_compare_fusion), kind=kOutput, calls=%fused_computation.6 | convolution fusion | flops 684195840 | bytes 21549056 | tf_op jit(solution)/shard_map/bstji,bsid->bstjd/dot_general | solution.py:76
  46.4 1.7 convolution_add_fusion
  48.1 1.3 dynamic-slice_bitcast_fusion.1
  49.4 1.2 collective-permute-start.3
  50.5 0.2 constant_dynamic-slice_fusion.2
  50.7 0.1 copy.41
  50.9 0.3 collective-permute-start.2
  51.2 6.7 %convert_reduce_fusion = f32[64,5,16]{2,1,0:T(8,128)S(1)} fusion(f32[64,5,16]{2,1,0:T(8,128)S(1)} %max.16, f32[64,5,16,512]{3,2,1,0:T(8,128)} %copy-done, pred[64,512]{1,0:T(8,128)(4,1)S(1)} %broadcast_compare_fusion), kind=kLoop, calls=%fused_computation.3 | loop fusion | flops 18344960 | bytes 10559488 | tf_op jit(solution)/shard_map/reduce_sum | solution.py:82
  57.9 0.2 constant_dynamic-slice_fusion.1
  58.3 1.2 collective-permute-start.4
  59.6 0.1 copy.44
  59.7 19.4 %collective-permute-done.2 = f32[64,1,5,8]{0,3,2,1:T(8,128)S(1)} collective-permute-done((f32[64,1,5,8]{0,3,2,1:T(8,128)S(1)}, f32[64,1,5,8]{0,3,2,1:T(8,128)S(1)}, u32[]{:S(2)}, u32[]{:S(2)}) %collective-permute-start.2) | collective-permute-done | bytes 10272 | tf_op jit(solution)/shard_map/ppermute | solution.py:16
  79.1 0.4 collective-permute-done.4
  79.5 0.2 copy.42
  79.7 0.1 copy.46
  79.9 1.0 fusion.8
  81.0 0.4 divide_convert_fusion
  81.4 1.0 copy.69
  82.4 0.2 all-reduce.2.cloned.1.call-start
  82.6 40.2 %all-gather.2.cloned.1.call-done = bf16[2560,1024]{1,0:T(8,128)(2,1)} async-done(((bf16[320,1024]{1,0:T(8,128)(2,1)}), bf16[2560,1024]{1,0:T(8,128)(2,1)}) %all-gather.2.cloned.1.call-update) | async-done | bytes 5242896 | tf_op jit(solution)/shard_map/all_gather | solution.py:124
  122.8 16.6 %convolution_convert_fusion = bf16[2560,2048]{1,0:T(8,128)(2,1)} fusion(bf16[2560,1024]{1,0:T(8,128)(2,1)} %all-gather.2.cloned.1.call-done, bf16[1024,2048]{1,0:T(8,128)(2,1)} %param.15), kind=kOutput, calls=%fused_computation | convolution fusion | flops 10742661120 | bytes 19922944 | tf_op jit(solution)/shard_map/dot_general | solution.py:123
  139.4 0.6 copy-done.4
  140.0 0.2 convert_reduce_fusion.2
  140.2 0.1 select_reduce_fusion
  140.3 0.7 all_to_all.9
  141.0 3.5 %all-to-all-start = ((s32[8,1,8]{2,1,0:T(1,128)}), s32[8,1,8]{2,1,0:T(1,128)S(1)}, u32[]{:S(2)}, u32[]{:S(2)}) async-start(s32[8,1,8]{2,1,0:T(1,128)} %bitcast.25), calls=%async_computation | async-start | bytes 8192 | tf_op jit(solution)/shard_map/all_to_all | solution.py:153
  144.7 0.1 broadcast_in_dim.102
  144.8 0.8 fusion.11
  145.6 3.4 %all-to-all-done = s32[8,1,8]{2,1,0:T(1,128)S(1)} async-done(((s32[8,1,8]{2,1,0:T(1,128)}), s32[8,1,8]{2,1,0:T(1,128)S(1)}, u32[]{:S(2)}, u32[]{:S(2)}) %all-to-all-start) | async-done | bytes 288 | tf_op jit(solution)/shard_map/all_to_all | solution.py:153
  149.0 4.0 %all-to-all-start.1 = ((bf16[8,8,640]{2,1,0:T(8,128)(2,1)}), bf16[8,8,640]{2,1,0:T(8,128)(2,1)S(1)}, u32[]{:S(2)}, u32[]{:S(2)}) async-start(bf16[8,8,640]{2,1,0:T(8,128)(2,1)} %fusion.11), calls=%async_computation.1 | async-start | bytes 163840 | tf_op jit(solution)/shard_map/all_to_all | solution.py:152
  153.0 0.5 broadcast.179
  153.5 0.7 reduce.9
  154.2 3.7 %all-to-all-done.1 = bf16[8,8,640]{2,1,0:T(8,128)(2,1)S(1)} async-done(((bf16[8,8,640]{2,1,0:T(8,128)(2,1)}), bf16[8,8,640]{2,1,0:T(8,128)(2,1)S(1)}, u32[]{:S(2)}, u32[]{:S(2)}) %all-to-all-start.1) | async-done | bytes 81952 | tf_op jit(solution)/shard_map/all_to_all | solution.py:152
  157.9 0.1 fusion.12
  158.1 0.7 copy.70
  158.7 139.5 %all-reduce.2.cloned.1.call-done = bf16[2560,2048]{1,0:T(8,128)(2,1)} async-done(((bf16[2560,2048]{1,0:T(8,128)(2,1)}), bf16[2560,2048]{1,0:T(8,128)(2,1)}) %all-reduce.2.cloned.1.call-update) | async-done | bytes 10485776 | tf_op jit(solution)/shard_map/psum | solution.py:129
  298.3 2.0 convert_convert_fusion
  (30 shorter events, 0.9 us)
Async XLA Ops:
  7.2 115.6 %all-gather.2.cloned.1.call-start = ((), (), s32[]{:S(2)}) async-start(), calls=%async_computation.2 | async-start | bytes 5898240 | tf_op jit(solution)/shard_map/all_gather | solution.py:124
  7.2 20.3 %collective-permute-start = (bf16[320,1024]{1,0:T(8,128)(2,1)}, bf16[320,1024]{1,0:T(8,128)(2,1)S(1)}, u32[]{:S(2)}, u32[]{:S(2)}) collective-permute-start(bf16[320,1024]{1,0:T(8,128)(2,1)} %param.8), channel_id=1, source_target_pairs={{0,1},{1,0},{2,3},{3,2},{4,5},{5,4},{6,7},{7,6},{8,9},{9,8},{10,11... | collective-permute-start | bytes 1966088 | tf_op jit(solution)/shard_map/ppermute | solution.py:16
  9.8 16.4 %collective-permute-start.1 = (bf16[320,128]{1,0:T(8,128)(2,1)}, bf16[320,128]{1,0:T(8,128)(2,1)S(1)}, u32[]{:S(2)}, u32[]{:S(2)}) collective-permute-start(bf16[320,128]{1,0:T(8,128)(2,1)} %param.9), channel_id=1, source_target_pairs={{0,1},{1,0},{2,3},{3,2},{4,5},{5,4},{6,7},{7,6},{8,9},{9,8},{10,11... | collective-permute-start | bytes 245768 | tf_op jit(solution)/shard_map/ppermute | solution.py:16
  36.1 10.3 %copy-start = (f32[64,5,16,512]{3,2,1,0:T(8,128)}, f32[64,5,16,512]{3,2,1,0:T(8,128)S(1)}, u32[]{:S(2)}) copy-start(f32[64,5,16,512]{3,2,1,0:T(8,128)S(1)} %get-tuple-element.27) | copy-start | bytes 31457284
  49.4 30.5 %collective-permute-start.3 = (f32[64,1,5,8,128]{4,3,2,0,1:T(8,128)}, f32[64,1,5,8,128]{4,3,2,0,1:T(8,128)S(1)}, u32[]{:S(2)}, u32[]{:S(2)}) collective-permute-start(f32[64,1,5,8,128]{4,3,2,0,1:T(8,128)} %get-tuple-element.17), channel_id=1, source_target_pairs={{0,1},{1,0},{2,3},{3,2},{4,5},{5,4},{6,7},{7,6},{8,9},{9,8},{10,11... | collective-permute-start | bytes 3932168 | tf_op jit(solution)/shard_map/ppermute | solution.py:16
  50.9 7.0 %copy-start.1 = (f32[64,5,16]{2,1,0:T(8,128)S(1)}, f32[64,5,16]{2,1,0:T(8,128)}, u32[]{:S(2)}) copy-start(f32[64,5,16]{2,1,0:T(8,128)} %convert_reduce_fusion.1) | copy-start | bytes 61444
  50.9 28.2 %collective-permute-start.2 = (f32[64,1,5,8]{0,3,2,1:T(8,128)S(1)}, f32[64,1,5,8]{0,3,2,1:T(8,128)S(1)}, u32[]{:S(2)}, u32[]{:S(2)}) collective-permute-start(f32[64,1,5,8]{0,3,2,1:T(8,128)S(1)} %bitcast.105), channel_id=1, source_target_pairs={{0,1},{1,0},{2,3},{3,2},{4,5},{5,4},{6,7},{7,6},{8,9},{9,8},{10,11... | collective-permute-start | bytes 30728 | tf_op jit(solution)/shard_map/ppermute | solution.py:16
  58.3 21.2 %collective-permute-start.4 = (f32[64,1,5,8]{0,3,2,1:T(8,128)S(1)}, f32[64,1,5,8]{0,3,2,1:T(8,128)S(1)}, u32[]{:S(2)}, u32[]{:S(2)}) collective-permute-start(f32[64,1,5,8]{0,3,2,1:T(8,128)S(1)} %bitcast.106), channel_id=1, source_target_pairs={{0,1},{1,0},{2,3},{3,2},{4,5},{5,4},{6,7},{7,6},{8,9},{9,8},{10,11... | collective-permute-start | bytes 30728 | tf_op jit(solution)/shard_map/ppermute | solution.py:16
  82.4 215.9 %all-reduce.2.cloned.1.call-start = ((), (), s32[]{:S(2)}) async-start(), calls=%async_computation.3 | async-start | bytes 20971520 | tf_op jit(solution)/shard_map/psum | solution.py:129
  139.4 0.7 copy-start.4
  139.4 5.1 %copy-start.2 = (bf16[320,128]{1,0:T(8,128)(2,1)S(1)}, bf16[320,128]{1,0:T(8,128)(2,1)}, u32[]{:S(2)}) copy-start(bf16[320,128]{1,0:T(8,128)(2,1)} %param.9) | copy-start | bytes 245764
  139.4 5.2 %copy-start.3 = (s32[64]{0:T(128)S(1)}, s32[64]{0:T(128)}, u32[]{:S(2)}) copy-start(s32[64]{0:T(128)} %param.13) | copy-start | bytes 772
  141.0 8.0 %all-to-all-start = ((s32[8,1,8]{2,1,0:T(1,128)}), s32[8,1,8]{2,1,0:T(1,128)S(1)}, u32[]{:S(2)}, u32[]{:S(2)}) async-start(s32[8,1,8]{2,1,0:T(1,128)} %bitcast.25), calls=%async_computation | async-start | bytes 8192 | tf_op jit(solution)/shard_map/all_to_all | solution.py:153
  149.0 8.9 %all-to-all-start.1 = ((bf16[8,8,640]{2,1,0:T(8,128)(2,1)}), bf16[8,8,640]{2,1,0:T(8,128)(2,1)S(1)}, u32[]{:S(2)}, u32[]{:S(2)}) async-start(bf16[8,8,640]{2,1,0:T(8,128)(2,1)} %fusion.11), calls=%async_computation.1 | async-start | bytes 163840 | tf_op jit(solution)/shard_map/all_to_all | solution.py:152
Sparse Core Ops, SparseCore 0:
  82.5 40.2 all-gather.1
  139.5 158.7 all-reduce.1
where the time goes:
time: 308 us; the launch traced here: 307 us
  waiting for transfers between devices  221 us (72%)
  matrix products  34.4 us (11%)
  other arithmetic  17.1 us (6%)
  between operations  14.3 us (5%)
  starting transfers between devices  13 us (4%)
  local copies, waits for them, and re-layouts  6.79 us (2%)
    psum x1, waiting for transfers between devices, shards(): totals = lax.psum(projected.astype(jnp.bfloat16), 'mp').astype(jnp.float32)  140 us
    all_gather x1, waiting for transfers between devices, shards(): lax.all_gather(attention, 'row', axis=0, tiled=True)  40.2 us
    ppermute x5, waiting for transfers between devices, partner(): return lax.ppermute(block, axis, route)  34.5 us
    dot_general x1, matrix products, shards(): jnp.dot(lax.all_gather(attention, 'row', axis=0, tiled=True), out_weight,...  16.6 us
    reduce_sum x1, other arithmetic, shards(): jnp.sum(cache_weights.astype(jnp.float32), -1)  6.68 us
    dot_general x1, matrix products, shards(): jnp.einsum('btjd,bsid->bstji', query_block, cache_keys, preferred_element...  6.47 us
  transfers between devices with their start and end apart: 9, of which 7 were waited for; matrix products, arithmetic and copies ran while one was open for 5% of the time, Pallas kernels for 0%

commit v1 on v0

--- a/solution.py
+++ b/solution.py
@@ -120,11 +120,10 @@
         .astype(jnp.bfloat16)
         .reshape(beams_here * drafts, heads_owned * head_size)
     )
-    projected = jnp.dot(
-        lax.all_gather(attention, "row", axis=0, tiled=True),
-        out_weight,
-        preferred_element_type=jnp.float32,
+    _rest_task = lambda content, dim_k: jnp.concatenate(
+        jax.lax.all_to_all(jnp.stack([content] * jax.lax.axis_size("row")), "row", 0, 0), dim_k
     )
+    projected = jnp.dot(_rest_task(attention, 0), out_weight, preferred_element_type=jnp.float32)
     rows_owned = projected.shape[0] // lax.axis_size("mp")
     totals = lax.psum(projected.astype(jnp.bfloat16), "mp").astype(jnp.float32)
     owned_rows = lax.dynamic_slice_in_dim(totals, mp_place * rows_owned, rows_owned, 0)

time: 308 us -> 332 us (1.078)
  blocking collectives: 0 us -> 67.2 us
  waiting for transfers between devices: 221 us -> 181 us
    all_to_all x0 -> x1, blocking collectives: none -> 67.2 us  [shards(): jax.lax.all_to_all(jnp.stack([content] * jax.lax.axis_size('row')), 'row'...]
    all_gather x1 -> x0, waiting for transfers between devices: 40.2 us -> none  [shards(): lax.all_gather(attention, 'row', axis=0, tiled=True)]
    dot_general x1, matrix products: 16.6 us -> 13.2 us  [shards(): jnp.dot(_rest_task(attention, 0), out_weight, preferred_element_type=jnp....]
  transfers between devices with their start and end apart: 9 -> 8, of which waited for: 7 -> 6; matrix products, arithmetic and copies ran while one was open for 5% -> 4% of each run, Pallas kernels for 0% -> 0%
where the time goes in v1:
time: 332 us; the launch traced here: 331 us
  waiting for transfers between devices  181 us (55%)
  blocking collectives  67.2 us (20%)
  matrix products  31.1 us (9%)
  other arithmetic  17.1 us (5%)
  between operations  14.3 us (4%)
  starting transfers between devices  13.6 us (4%)
  local copies, waits for them, and re-layouts  6.62 us (2%)
    psum x1, waiting for transfers between devices, shards(): totals = lax.psum(projected.astype(jnp.bfloat16), 'mp').astype(jnp.float32)  140 us
    all_to_all x1, blocking collectives, shards(): jax.lax.all_to_all(jnp.stack([content] * jax.lax.axis_size('row')), 'row'...  67.2 us
    ppermute x5, waiting for transfers between devices, partner(): return lax.ppermute(block, axis, route)  34.5 us
    dot_general x1, matrix products, shards(): jnp.dot(_rest_task(attention, 0), out_weight, preferred_element_type=jnp....  13.2 us
    reduce_sum x1, other arithmetic, shards(): jnp.sum(cache_weights.astype(jnp.float32), -1)  6.68 us
  transfers between devices with their start and end apart: 8, of which 6 were waited for; matrix products, arithmetic and copies ran while one was open for 4% of the time, Pallas kernels for 0%

profile of v1, /device:TPU:1, one launch (start us, length us, event | category | flops | bytes accessed | tf_op | source)
XLA Modules:
  0.0 331.1 jit_solution(8797938787377897587)
XLA Ops:
  7.2 2.5 collective-permute-start
  9.9 0.7 fusion.18
  10.7 0.7 broadcast_compare_fusion
  11.4 14.7 %collective-permute-done.1 = bf16[320,128]{1,0:T(8,128)(2,1)S(1)} collective-permute-done((bf16[320,128]{1,0:T(8,128)(2,1)}, bf16[320,128]{1,0:T(8,128)(2,1)S(1)}, u32[]{:S(2)}, u32[]{:S(2)}) %collective-permute-start.1) | collective-permute-done | bytes 81952 | tf_op jit(solution)/shard_map/ppermute | solution.py:16
  26.2 1.0 maximum_select_fusion.2
  27.2 0.2 fusion.26
  27.5 1.8 fusion.10
  29.3 0.3 copy.56
  29.6 6.5 %fusion.1 = (f32[64,5,16]{2,1,0:T(8,128)S(1)}, f32[64,5,16,512]{3,2,1,0:T(8,128)S(1)}) fusion(pred[64,512]{1,0:T(8,128)(4,1)S(1)} %broadcast_compare_fusion, bf16[64,5,16,128]{3,2,1,0:T(8,128)(2,1)S(1)} %bitcast.97, bf16[64,1,512,128]{3,2,1,0:T(8,128)(2,1)} %param.10), kind=kOutput, calls=%fused_computation.5 | convolution fusion | flops 678947840 | bytes 20238336 | tf_op jit(solution)/shard_map/btjd,bsid->bstji/dot_general | solution.py:52
  36.1 3.2 fusion.27
  39.3 1.5 convert_reduce_fusion.1
  40.8 5.6 %fusion.2 = f32[64,5,16,128]{3,2,1,0:T(8,128)S(1)} fusion(bf16[64,1,512,128]{3,2,1,0:T(8,128)(2,1)} %param.11, f32[64,5,16,512]{3,2,1,0:T(8,128)S(1)} %get-tuple-element.27, f32[64,5,16]{2,1,0:T(8,128)S(1)} %max.16, pred[64,512]{1,0:T(8,128)(4,1)S(1)} %broadcast_compare_fusion), kind=kOutput, calls=%fused_computation.6 | convolution fusion | flops 684195840 | bytes 21549056 | tf_op jit(solution)/shard_map/bstji,bsid->bstjd/dot_general | solution.py:76
  46.4 1.7 convolution_add_fusion
  48.1 1.3 dynamic-slice_bitcast_fusion.1
  49.4 1.2 collective-permute-start.3
  50.5 0.2 constant_dynamic-slice_fusion.2
  50.7 0.1 copy.41
  50.9 0.3 collective-permute-start.2
  51.2 6.7 %convert_reduce_fusion = f32[64,5,16]{2,1,0:T(8,128)S(1)} fusion(f32[64,5,16]{2,1,0:T(8,128)S(1)} %max.16, f32[64,5,16,512]{3,2,1,0:T(8,128)} %copy-done, pred[64,512]{1,0:T(8,128)(4,1)S(1)} %broadcast_compare_fusion), kind=kLoop, calls=%fused_computation.3 | loop fusion | flops 18344960 | bytes 10559488 | tf_op jit(solution)/shard_map/reduce_sum | solution.py:82
  57.9 0.2 constant_dynamic-slice_fusion.1
  58.3 1.2 collective-permute-start.4
  59.6 0.1 copy.44
  59.7 19.4 %collective-permute-done.2 = f32[64,1,5,8]{0,3,2,1:T(8,128)S(1)} collective-permute-done((f32[64,1,5,8]{0,3,2,1:T(8,128)S(1)}, f32[64,1,5,8]{0,3,2,1:T(8,128)S(1)}, u32[]{:S(2)}, u32[]{:S(2)}) %collective-permute-start.2) | collective-permute-done | bytes 10272 | tf_op jit(solution)/shard_map/ppermute | solution.py:16
  79.1 0.4 collective-permute-done.4
  79.5 0.2 copy.42
  79.7 0.1 copy.46
  79.9 1.0 fusion.8
  81.0 0.4 divide_convert_fusion
  81.4 0.1 copy.69
  81.5 0.7 stack.3
  82.2 67.2 %all_to_all.19 = bf16[8,320,1024]{2,1,0:T(8,128)(2,1)S(1)} all-to-all(bf16[8,320,1024]{2,1,0:T(8,128)(2,1)S(1)} %stack.3), channel_id=1, replica_groups=mesh['row'=8,'mp'=16] {'row'}, dimensions={0} | all-to-all | bytes 10485760 | tf_op jit(solution)/shard_map/all_to_all | solution.py:124
  149.3 13.2 %convolution_convert_fusion = bf16[2560,2048]{1,0:T(8,128)(2,1)} fusion(bf16[2560,1024]{1,0:T(8,128)(2,1)S(1)} %bitcast.99, bf16[1024,2048]{1,0:T(8,128)(2,1)S(1)} %copy-done.4), kind=kOutput, calls=%fused_computation | convolution fusion | flops 10742661120 | bytes 19922944 | tf_op jit(solution)/shard_map/dot_general | solution.py:126
  162.6 0.6 copy-done.5
  163.2 0.2 convert_reduce_fusion.2
  163.4 0.1 select_reduce_fusion
  163.5 0.7 all_to_all.13
  164.2 4.3 %all-to-all-start.1 = ((s32[8,1,8]{2,1,0:T(1,128)}), s32[8,1,8]{2,1,0:T(1,128)S(1)}, u32[]{:S(2)}, u32[]{:S(2)}) async-start(s32[8,1,8]{2,1,0:T(1,128)} %bitcast.26), calls=%async_computation.1 | async-start | bytes 8192 | tf_op jit(solution)/shard_map/all_to_all | solution.py:152
  168.6 0.1 broadcast_in_dim.102
  168.8 0.8 fusion.11
  169.6 3.4 %all-to-all-done.1 = s32[8,1,8]{2,1,0:T(1,128)S(1)} async-done(((s32[8,1,8]{2,1,0:T(1,128)}), s32[8,1,8]{2,1,0:T(1,128)S(1)}, u32[]{:S(2)}, u32[]{:S(2)}) %all-to-all-start.1) | async-done | bytes 288 | tf_op jit(solution)/shard_map/all_to_all | solution.py:152
  173.0 4.0 %all-to-all-start.2 = ((bf16[8,8,640]{2,1,0:T(8,128)(2,1)}), bf16[8,8,640]{2,1,0:T(8,128)(2,1)S(1)}, u32[]{:S(2)}, u32[]{:S(2)}) async-start(bf16[8,8,640]{2,1,0:T(8,128)(2,1)} %fusion.11), calls=%async_computation.2 | async-start | bytes 163840 | tf_op jit(solution)/shard_map/all_to_all | solution.py:151
  176.9 0.5 broadcast.181
  177.4 0.7 reduce.9
  178.2 3.7 %all-to-all-done.2 = bf16[8,8,640]{2,1,0:T(8,128)(2,1)S(1)} async-done(((bf16[8,8,640]{2,1,0:T(8,128)(2,1)}), bf16[8,8,640]{2,1,0:T(8,128)(2,1)S(1)}, u32[]{:S(2)}, u32[]{:S(2)}) %all-to-all-start.2) | async-done | bytes 81952 | tf_op jit(solution)/shard_map/all_to_all | solution.py:151
  181.9 0.1 fusion.12
  182.1 0.7 copy.70
  182.7 139.6 %all-reduce.2.cloned.1.call-done = bf16[2560,2048]{1,0:T(8,128)(2,1)} async-done(((bf16[2560,2048]{1,0:T(8,128)(2,1)}), bf16[2560,2048]{1,0:T(8,128)(2,1)}) %all-reduce.2.cloned.1.call-update) | async-done | bytes 10485776 | tf_op jit(solution)/shard_map/psum | solution.py:128
  322.3 2.0 convert_convert_fusion
  (31 shorter events, 0.8 us)
Async XLA Ops:
  7.2 315.1 %all-reduce.2.cloned.1.call-start = ((), (), s32[]{:S(2)}) async-start(), calls=%async_computation.3 | async-start | bytes 20971520 | tf_op jit(solution)/shard_map/psum | solution.py:128
  7.2 20.3 %collective-permute-start = (bf16[320,1024]{1,0:T(8,128)(2,1)}, bf16[320,1024]{1,0:T(8,128)(2,1)S(1)}, u32[]{:S(2)}, u32[]{:S(2)}) collective-permute-start(bf16[320,1024]{1,0:T(8,128)(2,1)} %param.8), channel_id=1, source_target_pairs={{0,1},{1,0},{2,3},{3,2},{4,5},{5,4},{6,7},{7,6},{8,9},{9,8},{10,11... | collective-permute-start | bytes 1966088 | tf_op jit(solution)/shard_map/ppermute | solution.py:16
  9.8 16.4 %collective-permute-start.1 = (bf16[320,128]{1,0:T(8,128)(2,1)}, bf16[320,128]{1,0:T(8,128)(2,1)S(1)}, u32[]{:S(2)}, u32[]{:S(2)}) collective-permute-start(bf16[320,128]{1,0:T(8,128)(2,1)} %param.9), channel_id=1, source_target_pairs={{0,1},{1,0},{2,3},{3,2},{4,5},{5,4},{6,7},{7,6},{8,9},{9,8},{10,11... | collective-permute-start | bytes 245768 | tf_op jit(solution)/shard_map/ppermute | solution.py:16
  36.1 10.3 %copy-start = (f32[64,5,16,512]{3,2,1,0:T(8,128)}, f32[64,5,16,512]{3,2,1,0:T(8,128)S(1)}, u32[]{:S(2)}) copy-start(f32[64,5,16,512]{3,2,1,0:T(8,128)S(1)} %get-tuple-element.27) | copy-start | bytes 31457284
  49.4 30.5 %collective-permute-start.3 = (f32[64,1,5,8,128]{4,3,2,0,1:T(8,128)}, f32[64,1,5,8,128]{4,3,2,0,1:T(8,128)S(1)}, u32[]{:S(2)}, u32[]{:S(2)}) collective-permute-start(f32[64,1,5,8,128]{4,3,2,0,1:T(8,128)} %get-tuple-element.17), channel_id=1, source_target_pairs={{0,1},{1,0},{2,3},{3,2},{4,5},{5,4},{6,7},{7,6},{8,9},{9,8},{10,11... | collective-permute-start | bytes 3932168 | tf_op jit(solution)/shard_map/ppermute | solution.py:16
  50.9 7.0 %copy-start.1 = (f32[64,5,16]{2,1,0:T(8,128)S(1)}, f32[64,5,16]{2,1,0:T(8,128)}, u32[]{:S(2)}) copy-start(f32[64,5,16]{2,1,0:T(8,128)} %convert_reduce_fusion.1) | copy-start | bytes 61444
  50.9 28.2 %collective-permute-start.2 = (f32[64,1,5,8]{0,3,2,1:T(8,128)S(1)}, f32[64,1,5,8]{0,3,2,1:T(8,128)S(1)}, u32[]{:S(2)}, u32[]{:S(2)}) collective-permute-start(f32[64,1,5,8]{0,3,2,1:T(8,128)S(1)} %bitcast.107), channel_id=1, source_target_pairs={{0,1},{1,0},{2,3},{3,2},{4,5},{5,4},{6,7},{7,6},{8,9},{9,8},{10,11... | collective-permute-start | bytes 30728 | tf_op jit(solution)/shard_map/ppermute | solution.py:16
  58.3 21.2 %collective-permute-start.4 = (f32[64,1,5,8]{0,3,2,1:T(8,128)S(1)}, f32[64,1,5,8]{0,3,2,1:T(8,128)S(1)}, u32[]{:S(2)}, u32[]{:S(2)}) collective-permute-start(f32[64,1,5,8]{0,3,2,1:T(8,128)S(1)} %bitcast.108), channel_id=1, source_target_pairs={{0,1},{1,0},{2,3},{3,2},{4,5},{5,4},{6,7},{7,6},{8,9},{9,8},{10,11... | collective-permute-start | bytes 30728 | tf_op jit(solution)/shard_map/ppermute | solution.py:16
  82.2 67.2 %copy-start.4 = (bf16[1024,2048]{1,0:T(8,128)(2,1)S(1)}, bf16[1024,2048]{1,0:T(8,128)(2,1)}, u32[]{:S(2)}) copy-start(bf16[1024,2048]{1,0:T(8,128)(2,1)} %param.15) | copy-start | bytes 12582916
  162.5 0.7 copy-start.5
  162.5 5.9 %copy-start.2 = (bf16[320,128]{1,0:T(8,128)(2,1)S(1)}, bf16[320,128]{1,0:T(8,128)(2,1)}, u32[]{:S(2)}) copy-start(bf16[320,128]{1,0:T(8,128)(2,1)} %param.9) | copy-start | bytes 245764
  162.6 6.0 %copy-start.3 = (s32[64]{0:T(128)S(1)}, s32[64]{0:T(128)}, u32[]{:S(2)}) copy-start(s32[64]{0:T(128)} %param.13) | copy-start | bytes 772
  164.2 8.8 %all-to-all-start.1 = ((s32[8,1,8]{2,1,0:T(1,128)}), s32[8,1,8]{2,1,0:T(1,128)S(1)}, u32[]{:S(2)}, u32[]{:S(2)}) async-start(s32[8,1,8]{2,1,0:T(1,128)} %bitcast.26), calls=%async_computation.1 | async-start | bytes 8192 | tf_op jit(solution)/shard_map/all_to_all | solution.py:152
  173.0 8.9 %all-to-all-start.2 = ((bf16[8,8,640]{2,1,0:T(8,128)(2,1)}), bf16[8,8,640]{2,1,0:T(8,128)(2,1)S(1)}, u32[]{:S(2)}, u32[]{:S(2)}) async-start(bf16[8,8,640]{2,1,0:T(8,128)(2,1)} %fusion.11), calls=%async_computation.2 | async-start | bytes 163840 | tf_op jit(solution)/shard_map/all_to_all | solution.py:151
Sparse Core Ops, SparseCore 0:
  162.7 159.5 all-reduce.1
